TPU v7x, 32 devices: a whole 2x2x4 slice. The times are simulated.
32 devices in a mesh: vol: 1, slab: 8 (over z, x), filt: 4 (over y, core).
Axes of the slice: x: 2, y: 2, z: 4, core: 2. Of those that a mesh axis runs over, the one named last changes fastest.
Arguments:
- volume: bfloat16 [32, 64, 64, 256], P(('vol', 'slab', 'filt')), may hold values from -6 to 6
- weights: bfloat16 [256, 27, 256], P('filt'), may hold values from -0.078125 to 0.078125
- bias: bfloat16 [256], P('filt'), may hold values from -3 to 3
Outputs:
- activated: bfloat16 [32, 64, 64, 256], P(('vol', 'slab'), None, None, 'filt')
All inputs are finite; a program needn't handle non-finite values.
Results may differ from a plain program's by a relative error of at most 0.001.
Values may be sent and summed in bfloat16 or wider, within the bound.
A program may use at most 448 MiB of HBM per device.

v0:
```python
import jax
import jax.numpy as jnp
from jax import lax
from jax.sharding import PartitionSpec as P


def extended(cells, sides, width):
    for axis, dim in sides:
        count = lax.axis_size(axis)
        ends = count - 1
        head = lax.slice_in_dim(cells, 0, width, axis=dim)
        tail = lax.slice_in_dim(cells, cells.shape[dim] - width, cells.shape[dim], axis=dim)
        cells = jnp.concatenate(
            [
                lax.ppermute(tail, axis, [(i, (i + 1) % count) for i in range(ends)]),
                cells,
                lax.ppermute(head, axis, [((i + 1) % count, i) for i in range(ends)]),
            ],
            axis=dim,
        )
    return cells


def convolve(padded, weights, bias):
    planes = padded.shape[0] - 2
    rows = padded.shape[1]
    cols = padded.shape[2]
    chans = padded.shape[3]
    outs = weights.shape[0]
    framed = jnp.pad(padded, ((0, 0), (1, 1), (1, 1), (0, 0)))
    total = jnp.zeros((planes, rows * cols, outs), jnp.float32)
    for tap_z in range(3):
        for tap_y in range(3):
            for tap_x in range(3):
                window = framed[
                    tap_z : tap_z + planes, tap_y : tap_y + rows, tap_x : tap_x + cols
                ].reshape(planes, rows * cols, chans)
                tap_weight = weights[:, 9 * tap_z + 3 * tap_y + tap_x, :]
                total = total + jnp.einsum(
                    "zpi,oi->zpo", window, tap_weight, preferred_element_type=jnp.float32
                )
    shifted = total + bias.astype(jnp.float32)[None, None, :]
    result = jnp.where(shifted > 0, shifted, 0.3 * shifted)
    return result.astype(jnp.bfloat16).reshape(planes, rows, cols, outs)


def body(volume, weights, bias):
    slab_planes = lax.all_gather(volume, "filt", axis=0, tiled=True)
    padded = extended(slab_planes, (("slab", 0),), 1)
    return convolve(padded, weights, bias)


def solution(mesh):
    return jax.shard_map(
        body,
        mesh=mesh,
        in_specs=(P(("vol", "slab", "filt"), None, None, None), P("filt", None, None), P("filt")),
        out_specs=P(("vol", "slab"), None, None, "filt"),
        check_vma=False,
    )
```

profile of v0, /device:TPU:0, one launch (start us, length us, event | category | flops | bytes accessed | tf_op | source)
XLA Modules:
  0.0 524.3 jit_solution(2084521685995472989)
XLA Ops:
  6.5 0.7 all-gather.2.cloned.1.call-update
  7.3 62.7 %all-gather.2.cloned.1.call-done = bf16[4,64,64,256]{3,2,1,0:T(8,128)(2,1)} async-done(((bf16[1,64,64,256]{3,2,1,0:T(8,128)(2,1)}), bf16[4,64,64,256]{3,2,1,0:T(8,128)(2,1)}) %all-gather.2.cloned.1.call-update) | async-done | bytes 8388624 | tf_op jit(solution)/shard_map/all_gather | solution.py:48
  69.9 2.9 fusion.113
  72.8 3.6 collective-permute-start
  76.5 1.3 collective-permute-start.1
  77.8 0.6 convert_element_type.8
  78.4 4.6 fusion.57
  82.9 83.6 %collective-permute-done = bf16[1,64,64,256]{3,2,1,0:T(8,128)(2,1)S(1)} collective-permute-done((bf16[1,64,64,256]{3,2,1,0:T(8,128)(2,1)S(1)}, bf16[1,64,64,256]{3,2,1,0:T(8,128)(2,1)S(1)}, u32[]{:S(2)}, u32[]{:S(2)}) %collective-permute-start) | collective-permute-done | bytes 2097184 | tf_op jit(solution)/shard_map/ppermute | solution.py:15
  166.6 1.3 copy-done.2
  167.9 1.4 copy-done.4
  169.3 21.5 %select_maximum_fusion = bf16[6,66,66,256]{3,2,1,0:T(8,128)(2,1)} fusion(bf16[1,64,64,256]{3,2,1,0:T(8,128)(2,1)S(1)} %collective-permute-done.1, bf16[4,64,64,256]{3,2,1,0:T(8,128)(2,1)S(1)} %copy-done, bf16[1,64,64,256]{3,2,1,0:T(8,128)(2,1)S(1)} %collective-permute-done), kind=kLoop, calls=%fused_computation.7 | loop fusion | flops 127125504 | bytes 25964544 | tf_op jit(solution)/shard_map/concatenate | solution.py:13
  190.8 126.1 %fusion.111 = (bf16[4,64,64,256]{3,2,1,0:T(8,128)(2,1)}, bf16[4,64,64,256]{3,2,1,0:T(8,128)(2,1)}, bf16[4,64,64,256]{3,2,1,0:T(8,128)(2,1)}, bf16[4,64,64,256]{3...) fusion(bf16[6,66,66,256]{3,2,1,0:T(8,128)(2,1)} %select_maximum, ...), kind=kLoop, calls=%fused_computation.122 | loop fusion | bytes 318767104 | tf_op jit(solution)/shard_map/slice | solution.py:35
  316.9 32.3 %fusion.112 = (bf16[4,64,64,256]{3,2,1,0:T(8,128)(2,1)}, bf16[4,64,64,256]{3,2,1,0:T(8,128)(2,1)}, bf16[4,64,64,256]{3,2,1,0:T(8,128)(2,1)}, bf16[4,64,64,256]{3,2,1,0:T(8,128)(2,1)}, bf16[4,64,64,256]{3,2,1,0:T(8,128)(2,1)}) fusion(bf16[6,66,66,256]{3,2,1,0:T(8,128)(2,1)} %select_maximum_fusion), kind=kLoop, calls=%fused_computation.123 | loop fusion | bytes 83886080 | tf_op jit(solution)/shard_map/slice | solution.py:35
  349.2 0.0 slice-start.34
  349.2 8.2 %fusion.59 = f32[4,4096,64]{1,2,0:T(8,128)} fusion(bf16[4,4096,256]{2,1,0:T(8,128)(2,1)} %bitcast.221, bf16[64,27,256]{2,0,1:T(8,128)(2,1)S(1)} %copy-done.6), kind=kOutput, calls=%fused_computation.70 | convolution fusion | flops 536870912 | bytes 12615680 | tf_op jit(solution)/shard_map/zpi,oi->zpo/dot_general | solution.py:39
  357.4 4.6 fusion.61
  362.1 0.0 slice-start.30
  362.1 4.7 fusion.63
  366.8 4.6 fusion.65
  371.5 0.0 slice-start.26
  371.5 4.7 fusion.67
  376.1 0.0 slice-start.24
  376.1 4.6 fusion.69
  380.7 0.0 slice-start.42
  380.7 4.7 fusion.71
  385.4 0.0 slice-start.40
  385.4 4.6 fusion.73
  390.0 4.7 fusion.77
  394.8 4.6 fusion.79
  399.4 0.0 copy-start.3
  399.4 4.8 fusion.81
  404.2 4.4 pad_maximum_fusion.1
  408.6 4.6 fusion.75
  413.2 4.6 fusion.34
  417.8 4.6 fusion.36
  422.4 4.6 fusion.38
  427.0 4.6 fusion.42
  431.6 4.6 fusion.44
  436.2 4.6 fusion.46
  440.8 4.6 fusion.48
  445.4 4.7 fusion.50
  450.2 4.6 fusion.52
  454.8 4.6 fusion.54
  459.3 4.7 fusion.32
  464.0 4.6 fusion.40
  468.6 24.2 %fusion.29 = f32[4,4096,64]{1,2,0:T(8,128)} fusion(f32[4,4096,64]{1,2,0:T(8,128)} %fusion.57, f32[4,4096,64]{1,2,0:T(8,128)} %fusion.59, f32[4,4096,64]{1,2,0:T(8,128)} %fusion.61, f32[4,4096,64]{1,2,0:T(8,128)} %fusion.63, f32[4,4096,64]{1,2,0:T(8,128)} %fusion.65, f32[4,4096,64]{1,2,0:T(8,128)} %fusion.67, f32[4,4096,64]{1,2,0:T(8,128)} %fusion.69, ...), kind=kOutput, calls=%fused_computation.40 | convolution fusion | flops 550502400 | bytes 67141632 | tf_op jit(solution)/shard_map/zpi,oi->zpo/dot_general | solution.py:39
  492.8 19.7 %fusion.31 = bf16[4,4096,64]{1,2,0:T(8,128)(2,1)} fusion(f32[4,4096,64]{1,2,0:T(8,128)} %fusion.32, f32[4,4096,64]{1,2,0:T(8,128)} %fusion.34, f32[4,4096,64]{1,2,0:T(8,128)} %fusion.36, f32[4,4096,64]{1,2,0:T(8,128)} %fusion.38, f32[4,4096,64]{1,2,0:T(8,128)} %fusion.40, f32[4,4096,64]{1,2,0:T(8,128)} %fusion.42, f32[4,4096,64]{1,2,0:T(8,128)} %fusion.44, ...), kind=kOutput, calls=%fused_computation.42 | convolution fusion | flops 555745280 | bytes 65044992 | tf_op jit(solution)/shard_map/zpi,oi->zpo/dot_general | solution.py:39
  512.5 4.8 copy.6
  (126 shorter events, 0.2 us)
Async XLA Ops:
  6.5 71.2 %copy-start.8 = (bf16[64]{0:T(256)(128)(2,1)S(1)}, bf16[64]{0:T(256)(128)(2,1)}, u32[]{:S(2)}) copy-start(bf16[64]{0:T(256)(128)(2,1)} %param.5) | copy-start | bytes 388
  6.5 71.8 %copy-start.6 = (bf16[64,27,256]{2,0,1:T(8,128)(2,1)S(1)}, bf16[64,27,256]{2,0,1:T(8,128)(2,1)}, u32[]{:S(2)}) copy-start(bf16[64,27,256]{2,0,1:T(8,128)(2,1)} %param.4) | copy-start | bytes 2654212
  6.5 63.4 %all-gather.2.cloned.1.call-start = ((), (), s32[]{:S(2)}) async-start(), calls=%async_computation | async-start | bytes 10485760 | tf_op jit(solution)/shard_map/all_gather | solution.py:48
  69.9 8.4 %copy-start = (bf16[4,64,64,256]{3,2,1,0:T(8,128)(2,1)S(1)}, bf16[4,64,64,256]{3,2,1,0:T(8,128)(2,1)}, u32[]{:S(2)}) copy-start(bf16[4,64,64,256]{3,2,1,0:T(8,128)(2,1)} %all-gather.2.cloned.1.call-done) | copy-start | bytes 25165828
  72.8 93.7 %collective-permute-start = (bf16[1,64,64,256]{3,2,1,0:T(8,128)(2,1)S(1)}, bf16[1,64,64,256]{3,2,1,0:T(8,128)(2,1)S(1)}, u32[]{:S(2)}, u32[]{:S(2)}) collective-permute-start(bf16[1,64,64,256]{3,2,1,0:T(8,128)(2,1)S(1)} %get-tuple-element.31), channel_id=1, source_target_pairs={{0,4},{4,8},{8,12},{12,16},{16,20},{20,24},{24,28},{1,5},{5,9},{9,... | collective-permute-start | bytes 6291464 | tf_op jit(solution)/shard_map/ppermute | solution.py:15
  76.5 90.1 %collective-permute-start.1 = (bf16[1,64,64,256]{3,2,1,0:T(8,128)(2,1)S(1)}, bf16[1,64,64,256]{3,2,1,0:T(8,128)(2,1)S(1)}, u32[]{:S(2)}, u32[]{:S(2)}) collective-permute-start(bf16[1,64,64,256]{3,2,1,0:T(8,128)(2,1)S(1)} %get-tuple-element.32), channel_id=1, source_target_pairs={{4,0},{8,4},{12,8},{16,12},{20,16},{24,20},{28,24},{5,1},{9,5},{13... | collective-permute-start | bytes 6291464 | tf_op jit(solution)/shard_map/ppermute | solution.py:17
  349.2 8.2 %copy-start.1 = (bf16[4,64,64,256]{3,2,1,0:T(8,128)(2,1)S(1)}, bf16[4,64,64,256]{3,2,1,0:T(8,128)(2,1)}, u32[]{:S(2)}) copy-start(bf16[4,64,64,256]{3,2,1,0:T(8,128)(2,1)} %get-tuple-element.17) | copy-start | bytes 25165828
  349.2 12.8 %slice-start.34 = ((s8[8388608]{0:T(1024)(128)(4,1)}), s8[4194304]{0:T(1024)(128)(4,1)S(1)}, s32[]{:S(2)}) async-start(s8[8388608]{0:T(1024)(128)(4,1)} %bitcast.214), calls=%async_computation.35 | async-start | bytes 8388608
  357.4 4.7 slice-start.35
  357.4 9.4 %slice-start.32 = ((s8[8388608]{0:T(1024)(128)(4,1)}), s8[4194304]{0:T(1024)(128)(4,1)S(1)}, s32[]{:S(2)}) async-start(s8[8388608]{0:T(1024)(128)(4,1)} %bitcast.211), calls=%async_computation.33 | async-start | bytes 8388608
  362.1 4.7 slice-start.33
  362.1 9.4 %slice-start.30 = ((s8[8388608]{0:T(1024)(128)(4,1)}), s8[4194304]{0:T(1024)(128)(4,1)S(1)}, s32[]{:S(2)}) async-start(s8[8388608]{0:T(1024)(128)(4,1)} %bitcast.208), calls=%async_computation.31 | async-start | bytes 8388608
  366.8 4.7 slice-start.31
  366.8 9.3 %slice-start.28 = ((s8[8388608]{0:T(1024)(128)(4,1)}), s8[4194304]{0:T(1024)(128)(4,1)S(1)}, s32[]{:S(2)}) async-start(s8[8388608]{0:T(1024)(128)(4,1)} %bitcast.205), calls=%async_computation.29 | async-start | bytes 8388608
  371.4 4.7 slice-start.29
  371.5 9.3 %slice-start.26 = ((s8[8388608]{0:T(1024)(128)(4,1)}), s8[4194304]{0:T(1024)(128)(4,1)S(1)}, s32[]{:S(2)}) async-start(s8[8388608]{0:T(1024)(128)(4,1)} %bitcast.202), calls=%async_computation.27 | async-start | bytes 8388608
  376.1 9.3 %slice-start.24 = ((s8[8388608]{0:T(1024)(128)(4,1)}), s8[4194304]{0:T(1024)(128)(4,1)S(1)}, s32[]{:S(2)}) async-start(s8[8388608]{0:T(1024)(128)(4,1)} %bitcast.199), calls=%async_computation.25 | async-start | bytes 8388608
  380.7 4.7 slice-start.25
  380.7 9.3 %slice-start.42 = ((s8[8388608]{0:T(1024)(128)(4,1)}), s8[4194304]{0:T(1024)(128)(4,1)S(1)}, s32[]{:S(2)}) async-start(s8[8388608]{0:T(1024)(128)(4,1)} %bitcast.228), calls=%async_computation.43 | async-start | bytes 8388608
  385.4 4.6 slice-start.43
  385.4 9.4 %slice-start.40 = ((s8[8388608]{0:T(1024)(128)(4,1)}), s8[4194304]{0:T(1024)(128)(4,1)S(1)}, s32[]{:S(2)}) async-start(s8[8388608]{0:T(1024)(128)(4,1)} %bitcast.225), calls=%async_computation.41 | async-start | bytes 8388608
  390.0 4.8 slice-start.41
  390.0 9.4 %slice-start.38 = ((s8[8388608]{0:T(1024)(128)(4,1)}), s8[4194304]{0:T(1024)(128)(4,1)S(1)}, s32[]{:S(2)}) async-start(s8[8388608]{0:T(1024)(128)(4,1)} %bitcast.222), calls=%async_computation.39 | async-start | bytes 8388608
  394.8 9.4 %slice-start = ((s8[8388608]{0:T(1024)(128)(4,1)}), s8[4194304]{0:T(1024)(128)(4,1)S(1)}, s32[]{:S(2)}) async-start(s8[8388608]{0:T(1024)(128)(4,1)} %bitcast.164), calls=%async_computation.1 | async-start | bytes 8388608
  399.4 4.8 slice-start.1
  399.4 4.8 copy-start.3
  399.4 4.8 copy-start.5
  399.4 13.8 %slice-start.22 = ((s8[8388608]{0:T(1024)(128)(4,1)}), s8[4194304]{0:T(1024)(128)(4,1)S(1)}, s32[]{:S(2)}) async-start(s8[8388608]{0:T(1024)(128)(4,1)} %bitcast.196), calls=%async_computation.23 | async-start | bytes 8388608
  404.2 9.0 %slice-start.23 = ((s8[8388608]{0:T(1024)(128)(4,1)}), s8[4194304]{0:T(1024)(128)(4,1)S(1)}, s32[]{:S(2)}) async-start(s8[8388608]{0:T(1024)(128)(4,1)} %bitcast.196), calls=%async_computation.24 | async-start | bytes 8388608
  408.6 9.2 %slice-start.20 = ((s8[8388608]{0:T(1024)(128)(4,1)}), s8[4194304]{0:T(1024)(128)(4,1)S(1)}, s32[]{:S(2)}) async-start(s8[8388608]{0:T(1024)(128)(4,1)} %bitcast.193), calls=%async_computation.21 | async-start | bytes 8388608
  413.2 9.2 %slice-start.18 = ((s8[8388608]{0:T(1024)(128)(4,1)}), s8[4194304]{0:T(1024)(128)(4,1)S(1)}, s32[]{:S(2)}) async-start(s8[8388608]{0:T(1024)(128)(4,1)} %bitcast.190), calls=%async_computation.19 | async-start | bytes 8388608
  417.8 4.6 slice-start.19
  417.8 9.2 %slice-start.16 = ((s8[8388608]{0:T(1024)(128)(4,1)}), s8[4194304]{0:T(1024)(128)(4,1)S(1)}, s32[]{:S(2)}) async-start(s8[8388608]{0:T(1024)(128)(4,1)} %bitcast.187), calls=%async_computation.17 | async-start | bytes 8388608
  422.4 9.2 %slice-start.14 = ((s8[8388608]{0:T(1024)(128)(4,1)}), s8[4194304]{0:T(1024)(128)(4,1)S(1)}, s32[]{:S(2)}) async-start(s8[8388608]{0:T(1024)(128)(4,1)} %bitcast.184), calls=%async_computation.15 | async-start | bytes 8388608
  427.0 9.2 %slice-start.10 = ((s8[8388608]{0:T(1024)(128)(4,1)}), s8[4194304]{0:T(1024)(128)(4,1)S(1)}, s32[]{:S(2)}) async-start(s8[8388608]{0:T(1024)(128)(4,1)} %bitcast.178), calls=%async_computation.11 | async-start | bytes 8388608
  431.6 4.6 slice-start.11
  431.6 9.2 %slice-start.8 = ((s8[8388608]{0:T(1024)(128)(4,1)}), s8[4194304]{0:T(1024)(128)(4,1)S(1)}, s32[]{:S(2)}) async-start(s8[8388608]{0:T(1024)(128)(4,1)} %bitcast.175), calls=%async_computation.9 | async-start | bytes 8388608
  436.2 9.2 %slice-start.6 = ((s8[8388608]{0:T(1024)(128)(4,1)}), s8[4194304]{0:T(1024)(128)(4,1)S(1)}, s32[]{:S(2)}) async-start(s8[8388608]{0:T(1024)(128)(4,1)} %bitcast.172), calls=%async_computation.7 | async-start | bytes 8388608
  440.8 9.3 %slice-start.4 = ((s8[8388608]{0:T(1024)(128)(4,1)}), s8[4194304]{0:T(1024)(128)(4,1)S(1)}, s32[]{:S(2)}) async-start(s8[8388608]{0:T(1024)(128)(4,1)} %bitcast.169), calls=%async_computation.5 | async-start | bytes 8388608
  445.4 4.8 slice-start.5
  445.4 9.4 %slice-start.2 = ((s8[8388608]{0:T(1024)(128)(4,1)}), s8[4194304]{0:T(1024)(128)(4,1)S(1)}, s32[]{:S(2)}) async-start(s8[8388608]{0:T(1024)(128)(4,1)} %bitcast.166), calls=%async_computation.3 | async-start | bytes 8388608
  450.2 4.6 slice-start.3
  450.2 9.2 %slice-start.12 = ((s8[8388608]{0:T(1024)(128)(4,1)}), s8[4194304]{0:T(1024)(128)(4,1)S(1)}, s32[]{:S(2)}) async-start(s8[8388608]{0:T(1024)(128)(4,1)} %bitcast.181), calls=%async_computation.13 | async-start | bytes 8388608
  454.8 9.2 %slice-start.36 = ((s8[8388608]{0:T(1024)(128)(4,1)}), s8[4194304]{0:T(1024)(128)(4,1)S(1)}, s32[]{:S(2)}) async-start(s8[8388608]{0:T(1024)(128)(4,1)} %bitcast.217), calls=%async_computation.37 | async-start | bytes 8388608
  459.3 4.7 slice-start.37
  464.0 28.8 %slice-start.44 = ((s8[8388608]{0:T(1024)(128)(4,1)}), s8[4194304]{0:T(1024)(128)(4,1)S(1)}, s32[]{:S(2)}) async-start(s8[8388608]{0:T(1024)(128)(4,1)} %bitcast.232), calls=%async_computation.45 | async-start | bytes 8388608
  468.6 24.2 %slice-start.45 = ((s8[8388608]{0:T(1024)(128)(4,1)}), s8[4194304]{0:T(1024)(128)(4,1)S(1)}, s32[]{:S(2)}) async-start(s8[8388608]{0:T(1024)(128)(4,1)} %bitcast.232), calls=%async_computation.46 | async-start | bytes 8388608
  468.6 24.2 %copy-start.7 = (f32[64]{0:T(128)S(1)}, f32[64]{0:T(128)}, u32[]{:S(2)}) copy-start(f32[64]{0:T(128)} %convert_element_type.8) | copy-start | bytes 772
  (10 other events, 39.4 us)
Sparse Core Ops, SparseCore 0:
  8.9 60.9 all-gather.1
where the time goes:
time: 527 us; the launch traced here: 524 us
  local copies, waits for them, and re-layouts  169 us (32%)
  matrix products  163 us (31%)
  waiting for transfers between devices  147 us (28%)
  other arithmetic  26.5 us (5%)
  between operations  14 us (3%)
    dot_general x27, matrix products, convolve(): jnp.einsum('zpi,oi->zpo', window, tap_weight, preferred_element_type=jnp....  163 us
    slice x2, local copies, waits for them, and re-layouts, convolve(): framed[tap_z:tap_z + planes, tap_y:tap_y + rows, tap_x:tap_x + cols]  158 us
    ppermute x1, waiting for transfers between devices, extended(): lax.ppermute(tail, axis, [(i, (i + 1) % count) for i in range(ends)])  83.6 us
    all_gather x1, waiting for transfers between devices, body(): slab_planes = lax.all_gather(volume, 'filt', axis=0, tiled=True)  62.7 us
    concatenate x2, other arithmetic, extended(): jnp.concatenate([lax.ppermute(tail, axis, [(i, (i + 1) % count) for i in...  25.9 us
  transfers between devices with their start and end apart: 3, of which 2 were waited for; matrix products, arithmetic and copies ran while one was open for 1% of the time, Pallas kernels for 0%

commit v1 on v0

--- a/solution.py
+++ b/solution.py
@@ -2,6 +2,18 @@
 import jax.numpy as jnp
 from jax import lax
 from jax.sharding import PartitionSpec as P
+
+
+def gather_by_bits(x, axis, dim):
+    ways, here, step = (lax.axis_size(axis), lax.axis_index(axis), x.shape[dim])
+    line, have = (x, 1)
+    while have < ways:
+        line = jnp.concatenate(
+            [line, lax.ppermute(line, axis, [(d, (d - have) % ways) for d in range(ways)])],
+            axis=dim,
+        )
+        have = 2 * have
+    return jnp.roll(line, here * step, axis=dim)
 
 
 def extended(cells, sides, width):
@@ -45,7 +57,7 @@
 
 
 def body(volume, weights, bias):
-    slab_planes = lax.all_gather(volume, "filt", axis=0, tiled=True)
+    slab_planes = gather_by_bits(volume, "filt", 0)
     padded = extended(slab_planes, (("slab", 0),), 1)
     return convolve(padded, weights, bias)
 

time: 527 us -> 585 us (1.11)
  waiting for transfers between devices: 147 us -> 186 us
  local copies, waits for them, and re-layouts: 169 us -> 191 us
  between operations: 14 us -> 0.63 us
    ppermute x0 -> x2, waiting for transfers between devices: none -> 115 us  [gather_by_bits(): lax.ppermute(line, axis, [(d, (d - have) % ways) for d in range(ways)])]
    all_gather x1 -> x0, waiting for transfers between devices: 62.7 us -> none  [body(): slab_planes = lax.all_gather(volume, 'filt', axis=0, tiled=True)]
    ppermute x1, waiting for transfers between devices: 83.6 us -> 71.6 us  [extended(): lax.ppermute(tail, axis, [(i, (i + 1) % count) for i in range(ends)])]
    unnamed x110 -> x113, local copies, waits for them, and re-layouts: 2.95 us -> 13.5 us
    dynamic_slice x0 -> x1, local copies, waits for them, and re-layouts: none -> 8.36 us  [gather_by_bits(): return jnp.roll(line, here * step, axis=dim)]
  transfers between devices with their start and end apart: 3 -> 4, of which waited for: 2 -> 3; matrix products, arithmetic and copies ran while one was open for 1% -> 3% of each run, Pallas kernels for 0% -> 0%
where the time goes in v1:
time: 585 us; the launch traced here: 582 us
  local copies, waits for them, and re-layouts  191 us (33%)
  waiting for transfers between devices  186 us (32%)
  matrix products  164 us (28%)
  other arithmetic  31.7 us (5%)
  starting transfers between devices  8.03 us (1%)
    dot_general x27, matrix products, convolve(): jnp.einsum('zpi,oi->zpo', window, tap_weight, preferred_element_type=jnp....  164 us
    slice x2, local copies, waits for them, and re-layouts, convolve(): framed[tap_z:tap_z + planes, tap_y:tap_y + rows, tap_x:tap_x + cols]  161 us
    ppermute x2, waiting for transfers between devices, gather_by_bits(): lax.ppermute(line, axis, [(d, (d - have) % ways) for d in range(ways)])  115 us
    ppermute x1, waiting for transfers between devices, extended(): lax.ppermute(tail, axis, [(i, (i + 1) % count) for i in range(ends)])  71.6 us
    concatenate x2, other arithmetic, extended(): jnp.concatenate([lax.ppermute(tail, axis, [(i, (i + 1) % count) for i in...  27.2 us
    unnamed x113, local copies, waits for them, and re-layouts  13.5 us
  transfers between devices with their start and end apart: 4, of which 3 were waited for; matrix products, arithmetic and copies ran while one was open for 3% of the time, Pallas kernels for 0%

profile of v1, /device:TPU:0, one launch (start us, length us, event | category | flops | bytes accessed | tf_op | source)
XLA Modules:
  0.0 582.0 jit_solution(15041806501074869368)
XLA Ops:
  0.0 2.4 collective-permute-start
  2.4 23.9 %collective-permute-done = bf16[1,64,64,256]{3,2,1,0:T(8,128)(2,1)S(1)} collective-permute-done((bf16[1,64,64,256]{3,2,1,0:T(8,128)(2,1)}, bf16[1,64,64,256]{3,2,1,0:T(8,128)(2,1)S(1)}, u32[]{:S(2)}, u32[]{:S(2)}) %collective-permute-start) | collective-permute-done | bytes 2097184 | tf_op jit(solution)/shard_map/ppermute | solution.py:12
  26.3 1.3 copy-done.2
  27.6 4.0 pad_maximum_fusion.2
  31.6 0.6 collective-permute-start.1
  32.4 1.9 constant_dynamic-update-slice_fusion.4
  34.3 90.9 %collective-permute-done.1 = bf16[2,64,64,256]{3,2,1,0:T(8,128)(2,1)} collective-permute-done((bf16[2,64,64,256]{3,2,1,0:T(8,128)(2,1)}, bf16[2,64,64,256]{3,2,1,0:T(8,128)(2,1)}, u32[]{:S(2)}, u32[]{:S(2)}) %collective-permute-start.1) | collective-permute-done | bytes 4194336 | tf_op jit(solution)/shard_map/ppermute | solution.py:12
  125.2 2.5 constant_dynamic-update-slice_fusion.3
  128.1 2.5 constant_dynamic-update-slice_fusion
  130.6 5.8 copy-done.4
  136.4 2.4 constant_dynamic-slice_fusion.1
  138.8 3.5 collective-permute-start.2
  142.3 1.5 collective-permute-start.3
  144.3 8.4 %constant_dynamic-slice_fusion.2 = bf16[4,64,64,256]{3,2,1,0:T(8,128)(2,1)} fusion(bf16[8,64,64,256]{3,2,1,0:T(8,128)(2,1)} %copy-done.4, s32[]{:T(128)S(6)} %select_n.18), kind=kLoop, calls=%fused_computation.132 | loop fusion | bytes 16777220 | tf_op jit(solution)/shard_map/jit(_roll_dynamic)/dynamic_slice | solution.py:16
  152.7 8.1 %fusion.59 = f32[4,4096,64]{1,2,0:T(8,128)} fusion(bf16[4,4096,256]{2,1,0:T(8,128)(2,1)} %bitcast.163, bf16[64,27,256]{2,0,1:T(8,128)(2,1)S(1)} %copy-done.7), kind=kOutput, calls=%fused_computation.70 | convolution fusion | flops 536870912 | bytes 12615680 | tf_op jit(solution)/shard_map/zpi,oi->zpo/dot_general | solution.py:51
  160.8 71.6 %collective-permute-done.2 = bf16[1,64,64,256]{3,2,1,0:T(8,128)(2,1)S(1)} collective-permute-done((bf16[1,64,64,256]{3,2,1,0:T(8,128)(2,1)}, bf16[1,64,64,256]{3,2,1,0:T(8,128)(2,1)S(1)}, u32[]{:S(2)}, u32[]{:S(2)}) %collective-permute-start.2) | collective-permute-done | bytes 2097184 | tf_op jit(solution)/shard_map/ppermute | solution.py:27
  232.4 1.3 copy-done.5
  233.7 21.4 %select_maximum_fusion = bf16[6,66,66,256]{3,2,1,0:T(8,128)(2,1)} fusion(bf16[1,64,64,256]{3,2,1,0:T(8,128)(2,1)S(1)} %collective-permute-done.3, bf16[4,64,64,256]{3,2,1,0:T(8,128)(2,1)S(1)} %copy-done, bf16[1,64,64,256]{3,2,1,0:T(8,128)(2,1)S(1)} %collective-permute-done.2), kind=kLoop, calls=%fused_computation.7 | loop fusion | flops 127125504 | bytes 25964544 | tf_op jit(solution)/shard_map/concatenate | solution.py:25
  255.1 125.7 %fusion.113 = (bf16[4,64,64,256]{3,2,1,0:T(8,128)(2,1)}, bf16[4,64,64,256]{3,2,1,0:T(8,128)(2,1)}, bf16[4,64,64,256]{3,2,1,0:T(8,128)(2,1)}, bf16[4,64,64,256]{3...) fusion(bf16[6,66,66,256]{3,2,1,0:T(8,128)(2,1)} %select_maximum, ...), kind=kLoop, calls=%fused_computation.133 | loop fusion | bytes 318767104 | tf_op jit(solution)/shard_map/slice | solution.py:47
  380.8 35.6 %fusion.114 = (bf16[4,64,64,256]{3,2,1,0:T(8,128)(2,1)}, bf16[4,64,64,256]{3,2,1,0:T(8,128)(2,1)}, bf16[4,64,64,256]{3,2,1,0:T(8,128)(2,1)}, bf16[4,64,64,256]{3,2,1,0:T(8,128)(2,1)}, bf16[4,64,64,256]{3,2,1,0:T(8,128)(2,1)}) fusion(bf16[6,66,66,256]{3,2,1,0:T(8,128)(2,1)} %select_maximum_fusion), kind=kLoop, calls=%fused_computation.134 | loop fusion | bytes 83886080 | tf_op jit(solution)/shard_map/slice | solution.py:47
  416.4 5.8 pad_maximum_fusion.1
  422.2 4.6 fusion.41
  426.8 4.6 fusion.77
  431.4 4.6 fusion.35
  436.0 4.6 fusion.37
  440.7 4.6 fusion.39
  445.3 4.6 fusion.43
  450.0 4.6 fusion.45
  454.6 4.6 fusion.47
  459.2 4.9 fusion.49
  464.1 4.6 fusion.51
  468.8 4.6 fusion.53
  473.4 4.6 fusion.55
  478.0 4.7 fusion.57
  482.7 4.6 fusion.61
  487.3 4.6 fusion.63
  491.9 4.6 fusion.65
  496.5 4.6 fusion.67
  501.1 4.8 fusion.69
  505.9 4.6 fusion.71
  510.5 4.7 fusion.73
  515.2 8.2 %fusion.33 = f32[4,4096,64]{1,2,0:T(8,128)} fusion(bf16[4,4096,256]{2,1,0:T(8,128)(2,1)} %bitcast.182, bf16[64,27,256]{2,0,1:T(8,128)(2,1)S(1)} %copy-done.7), kind=kOutput, calls=%fused_computation.44 | convolution fusion | flops 536870912 | bytes 12615680 | tf_op jit(solution)/shard_map/zpi,oi->zpo/dot_general | solution.py:51
  523.4 4.6 fusion.75
  528.0 4.6 fusion.79
  532.6 4.6 fusion.81
  537.2 4.7 fusion.83
  541.9 36.7 %fusion.32 = bf16[4,4096,64]{1,2,0:T(8,128)(2,1)S(1)} fusion(f32[4,4096,64]{1,2,0:T(8,128)} %fusion.33, f32[4,4096,64]{1,2,0:T(8,128)} %fusion.35, f32[4,4096,64]{1,2,0:T(8,128)} %fusion.37, f32[4,4096,64]{1,2,0:T(8,128)} %fusion.39, f32[4,4096,64]{1,2,0:T(8,128)} %fusion.41, f32[4,4096,64]{1,2,0:T(8,128)} %fusion.43, f32[4,4096,64]{1,2,0:T(8,128)} %fusion.45, ...), kind=kOutput, calls=%fused_computation.42 | convolution fusion | flops 569376768 | bytes 119570944 | tf_op jit(solution)/shard_map/zpi,oi->zpo/dot_general | solution.py:51
  578.6 3.1 copy.5
  (132 shorter events, 1.3 us)
Async XLA Ops:
  0.0 32.2 %copy-start.1 = (bf16[1,64,64,256]{3,2,1,0:T(8,128)(2,1)S(1)}, bf16[1,64,64,256]{3,2,1,0:T(8,128)(2,1)}, u32[]{:S(2)}) copy-start(bf16[1,64,64,256]{3,2,1,0:T(8,128)(2,1)} %param.3) | copy-start | bytes 6291460
  0.0 26.3 %collective-permute-start = (bf16[1,64,64,256]{3,2,1,0:T(8,128)(2,1)}, bf16[1,64,64,256]{3,2,1,0:T(8,128)(2,1)S(1)}, u32[]{:S(2)}, u32[]{:S(2)}) collective-permute-start(bf16[1,64,64,256]{3,2,1,0:T(8,128)(2,1)} %param.3), channel_id=1, source_target_pairs={{0,3},{1,0},{2,1},{3,2},{4,7},{5,4},{6,5},{7,6},{8,11},{9,8},{10,9... | collective-permute-start | bytes 6291464 | tf_op jit(solution)/shard_map/ppermute | solution.py:12
  31.6 93.6 %collective-permute-start.1 = (bf16[2,64,64,256]{3,2,1,0:T(8,128)(2,1)}, bf16[2,64,64,256]{3,2,1,0:T(8,128)(2,1)}, u32[]{:S(2)}, u32[]{:S(2)}) collective-permute-start(bf16[2,64,64,256]{3,2,1,0:T(8,128)(2,1)} %pad_maximum_fusion.2), channel_id=1, source_target_pairs={{0,2},{1,3},{2,0},{3,1},{4,6},{5,7},{6,4},{7,5},{8,10},{9,11},{10,... | collective-permute-start | bytes 12582920 | tf_op jit(solution)/shard_map/ppermute | solution.py:12
  32.4 95.5 %copy-start.3 = (bf16[1,64,64,256]{3,2,1,0:T(8,128)(2,1)S(1)}, bf16[1,64,64,256]{3,2,1,0:T(8,128)(2,1)}, u32[]{:S(2)}) copy-start(bf16[1,64,64,256]{3,2,1,0:T(8,128)(2,1)} %copy-done.2) | copy-start | bytes 6291460
  128.1 15.7 %copy-start.9 = (bf16[64]{0:T(256)(128)(2,1)S(1)}, bf16[64]{0:T(256)(128)(2,1)}, u32[]{:S(2)}) copy-start(bf16[64]{0:T(256)(128)(2,1)} %param.5) | copy-start | bytes 388
  130.6 5.8 copy-start.4
  138.8 93.6 %collective-permute-start.2 = (bf16[1,64,64,256]{3,2,1,0:T(8,128)(2,1)}, bf16[1,64,64,256]{3,2,1,0:T(8,128)(2,1)S(1)}, u32[]{:S(2)}, u32[]{:S(2)}) collective-permute-start(bf16[1,64,64,256]{3,2,1,0:T(8,128)(2,1)} %get-tuple-element.5), channel_id=1, source_target_pairs={{0,4},{4,8},{8,12},{12,16},{16,20},{20,24},{24,28},{1,5},{5,9},{9,... | collective-permute-start | bytes 6291464 | tf_op jit(solution)/shard_map/ppermute | solution.py:27
  142.3 90.1 %collective-permute-start.3 = (bf16[1,64,64,256]{3,2,1,0:T(8,128)(2,1)}, bf16[1,64,64,256]{3,2,1,0:T(8,128)(2,1)S(1)}, u32[]{:S(2)}, u32[]{:S(2)}) collective-permute-start(bf16[1,64,64,256]{3,2,1,0:T(8,128)(2,1)} %get-tuple-element.6), channel_id=1, source_target_pairs={{4,0},{8,4},{12,8},{16,12},{20,16},{24,20},{28,24},{5,1},{9,5},{13... | collective-permute-start | bytes 6291464 | tf_op jit(solution)/shard_map/ppermute | solution.py:29
  144.3 8.4 %copy-start.7 = (bf16[64,27,256]{2,0,1:T(8,128)(2,1)S(1)}, bf16[64,27,256]{2,0,1:T(8,128)(2,1)}, u32[]{:S(2)}) copy-start(bf16[64,27,256]{2,0,1:T(8,128)(2,1)} %param.4) | copy-start | bytes 2654212
  152.7 81.0 %copy-start = (bf16[4,64,64,256]{3,2,1,0:T(8,128)(2,1)S(1)}, bf16[4,64,64,256]{3,2,1,0:T(8,128)(2,1)}, u32[]{:S(2)}) copy-start(bf16[4,64,64,256]{3,2,1,0:T(8,128)(2,1)} %constant_dynamic-slice_fusion.2) | copy-start | bytes 25165828
  380.8 35.6 %copy-start.6 = (bf16[1,64,64,256]{3,2,1,0:T(8,128)(2,1)S(1)}, bf16[1,64,64,256]{3,2,1,0:T(8,128)(2,1)}, u32[]{:S(2)}) copy-start(bf16[1,64,64,256]{3,2,1,0:T(8,128)(2,1)} %copy-done.5) | copy-start | bytes 6291460
  422.2 9.2 %slice-start.42 = ((s8[8388608]{0:T(1024)(128)(4,1)}), s8[4194304]{0:T(1024)(128)(4,1)S(1)}, s32[]{:S(2)}) async-start(s8[8388608]{0:T(1024)(128)(4,1)} %bitcast.228), calls=%async_computation.42 | async-start | bytes 8388608
  426.8 9.2 %slice-start.40 = ((s8[8388608]{0:T(1024)(128)(4,1)}), s8[4194304]{0:T(1024)(128)(4,1)S(1)}, s32[]{:S(2)}) async-start(s8[8388608]{0:T(1024)(128)(4,1)} %bitcast.225), calls=%async_computation.40 | async-start | bytes 8388608
  431.4 4.6 slice-start.41
  431.4 9.2 %slice-start.38 = ((s8[8388608]{0:T(1024)(128)(4,1)}), s8[4194304]{0:T(1024)(128)(4,1)S(1)}, s32[]{:S(2)}) async-start(s8[8388608]{0:T(1024)(128)(4,1)} %bitcast.222), calls=%async_computation.38 | async-start | bytes 8388608
  436.0 4.6 slice-start.39
  436.0 9.3 %slice-start.36 = ((s8[8388608]{0:T(1024)(128)(4,1)}), s8[4194304]{0:T(1024)(128)(4,1)S(1)}, s32[]{:S(2)}) async-start(s8[8388608]{0:T(1024)(128)(4,1)} %bitcast.219), calls=%async_computation.36 | async-start | bytes 8388608
  440.6 4.7 slice-start.37
  440.6 9.3 %slice-start.34 = ((s8[8388608]{0:T(1024)(128)(4,1)}), s8[4194304]{0:T(1024)(128)(4,1)S(1)}, s32[]{:S(2)}) async-start(s8[8388608]{0:T(1024)(128)(4,1)} %bitcast.216), calls=%async_computation.34 | async-start | bytes 8388608
  445.3 4.6 slice-start.35
  445.3 9.2 %slice-start.32 = ((s8[8388608]{0:T(1024)(128)(4,1)}), s8[4194304]{0:T(1024)(128)(4,1)S(1)}, s32[]{:S(2)}) async-start(s8[8388608]{0:T(1024)(128)(4,1)} %bitcast.213), calls=%async_computation.32 | async-start | bytes 8388608
  450.0 9.3 %slice-start.30 = ((s8[8388608]{0:T(1024)(128)(4,1)}), s8[4194304]{0:T(1024)(128)(4,1)S(1)}, s32[]{:S(2)}) async-start(s8[8388608]{0:T(1024)(128)(4,1)} %bitcast.210), calls=%async_computation.30 | async-start | bytes 8388608
  454.6 4.7 slice-start.31
  454.6 9.5 %slice-start.28 = ((s8[8388608]{0:T(1024)(128)(4,1)}), s8[4194304]{0:T(1024)(128)(4,1)S(1)}, s32[]{:S(2)}) async-start(s8[8388608]{0:T(1024)(128)(4,1)} %bitcast.207), calls=%async_computation.28 | async-start | bytes 8388608
  459.2 4.9 slice-start.29
  459.2 9.5 %slice-start.26 = ((s8[8388608]{0:T(1024)(128)(4,1)}), s8[4194304]{0:T(1024)(128)(4,1)S(1)}, s32[]{:S(2)}) async-start(s8[8388608]{0:T(1024)(128)(4,1)} %bitcast.204), calls=%async_computation.26 | async-start | bytes 8388608
  464.1 4.6 slice-start.27
  464.1 9.2 %slice-start.24 = ((s8[8388608]{0:T(1024)(128)(4,1)}), s8[4194304]{0:T(1024)(128)(4,1)S(1)}, s32[]{:S(2)}) async-start(s8[8388608]{0:T(1024)(128)(4,1)} %bitcast.201), calls=%async_computation.24 | async-start | bytes 8388608
  468.7 9.2 %slice-start.22 = ((s8[8388608]{0:T(1024)(128)(4,1)}), s8[4194304]{0:T(1024)(128)(4,1)S(1)}, s32[]{:S(2)}) async-start(s8[8388608]{0:T(1024)(128)(4,1)} %bitcast.198), calls=%async_computation.22 | async-start | bytes 8388608
  473.4 9.3 %slice-start.20 = ((s8[8388608]{0:T(1024)(128)(4,1)}), s8[4194304]{0:T(1024)(128)(4,1)S(1)}, s32[]{:S(2)}) async-start(s8[8388608]{0:T(1024)(128)(4,1)} %bitcast.195), calls=%async_computation.20 | async-start | bytes 8388608
  478.0 4.7 slice-start.21
  478.0 9.3 %slice-start.18 = ((s8[8388608]{0:T(1024)(128)(4,1)}), s8[4194304]{0:T(1024)(128)(4,1)S(1)}, s32[]{:S(2)}) async-start(s8[8388608]{0:T(1024)(128)(4,1)} %bitcast.192), calls=%async_computation.18 | async-start | bytes 8388608
  482.7 4.6 slice-start.19
  482.7 9.2 %slice-start.16 = ((s8[8388608]{0:T(1024)(128)(4,1)}), s8[4194304]{0:T(1024)(128)(4,1)S(1)}, s32[]{:S(2)}) async-start(s8[8388608]{0:T(1024)(128)(4,1)} %bitcast.189), calls=%async_computation.16 | async-start | bytes 8388608
  487.3 9.2 %slice-start.14 = ((s8[8388608]{0:T(1024)(128)(4,1)}), s8[4194304]{0:T(1024)(128)(4,1)S(1)}, s32[]{:S(2)}) async-start(s8[8388608]{0:T(1024)(128)(4,1)} %bitcast.186), calls=%async_computation.14 | async-start | bytes 8388608
  491.9 9.2 %slice-start.12 = ((s8[8388608]{0:T(1024)(128)(4,1)}), s8[4194304]{0:T(1024)(128)(4,1)S(1)}, s32[]{:S(2)}) async-start(s8[8388608]{0:T(1024)(128)(4,1)} %bitcast.183), calls=%async_computation.12 | async-start | bytes 8388608
  496.5 4.6 slice-start.13
  496.5 9.5 %slice-start.10 = ((s8[8388608]{0:T(1024)(128)(4,1)}), s8[4194304]{0:T(1024)(128)(4,1)S(1)}, s32[]{:S(2)}) async-start(s8[8388608]{0:T(1024)(128)(4,1)} %bitcast.179), calls=%async_computation.10 | async-start | bytes 8388608
  501.1 4.8 slice-start.11
  501.1 9.4 %slice-start.6 = ((s8[8388608]{0:T(1024)(128)(4,1)}), s8[4194304]{0:T(1024)(128)(4,1)S(1)}, s32[]{:S(2)}) async-start(s8[8388608]{0:T(1024)(128)(4,1)} %bitcast.173), calls=%async_computation.6 | async-start | bytes 8388608
  510.5 12.8 %slice-start.8 = ((s8[8388608]{0:T(1024)(128)(4,1)}), s8[4194304]{0:T(1024)(128)(4,1)S(1)}, s32[]{:S(2)}) async-start(s8[8388608]{0:T(1024)(128)(4,1)} %bitcast.176), calls=%async_computation.8 | async-start | bytes 8388608
  515.2 8.2 %slice-start.9 = ((s8[8388608]{0:T(1024)(128)(4,1)}), s8[4194304]{0:T(1024)(128)(4,1)S(1)}, s32[]{:S(2)}) async-start(s8[8388608]{0:T(1024)(128)(4,1)} %bitcast.176), calls=%async_computation.9 | async-start | bytes 8388608
  515.2 12.8 %slice-start.4 = ((s8[8388608]{0:T(1024)(128)(4,1)}), s8[4194304]{0:T(1024)(128)(4,1)S(1)}, s32[]{:S(2)}) async-start(s8[8388608]{0:T(1024)(128)(4,1)} %bitcast.170), calls=%async_computation.4 | async-start | bytes 8388608
  523.4 9.2 %slice-start.2 = ((s8[8388608]{0:T(1024)(128)(4,1)}), s8[4194304]{0:T(1024)(128)(4,1)S(1)}, s32[]{:S(2)}) async-start(s8[8388608]{0:T(1024)(128)(4,1)} %bitcast.167), calls=%async_computation.2 | async-start | bytes 8388608
  528.0 4.6 slice-start.3
  528.0 9.3 %slice-start = ((s8[8388608]{0:T(1024)(128)(4,1)}), s8[4194304]{0:T(1024)(128)(4,1)S(1)}, s32[]{:S(2)}) async-start(s8[8388608]{0:T(1024)(128)(4,1)} %bitcast.164), calls=%async_computation | async-start | bytes 8388608
  532.6 4.6 slice-start.1
  537.2 4.7 copy-start.8
  (10 other events, 39.5 us)
